TPU v7x, 256 devices: a whole 4x4x8 slice. The times are simulated.
256 devices in a mesh: group: 8 (over x, core), prompt: 32 (over z, y).
Axes of the slice: x: 4, y: 4, z: 8, core: 2. Of those that a mesh axis runs over, the one named last changes fastest.
Arguments:
- queries: bfloat16 [32, 8, 64, 3072], P('prompt', 'group'), may hold values from -48 to 48
- fresh_latent: bfloat16 [32, 8, 64, 576], P('prompt', 'group'), may hold values from -6 to 6
- latent_cache: bfloat16 [32, 8, 512, 576], P('prompt', 'group'), may hold values from -48 to 48
- selected: int32 [32, 8, 64], P('prompt', 'group'), may hold values from 0 to 511, as said below
- position: int32 [32, 8], P('prompt'), may hold values from 0 to 7, each once within a row
- latent_gain: bfloat16 [512], replicated, may hold values from 0.099609375 to 1.8984375
- kv_up: bfloat16 [512, 4096], P('prompt'), may hold values from -0.25 to 0.25
- out_weight: bfloat16 [2048, 2048], P('prompt'), may hold values from -0.125 to 0.125
Outputs:
- attended: bfloat16 [32, 8, 64, 2048], P('prompt', 'group')
- blended: bfloat16 [32, 8, 512, 576], P('prompt', 'group')
Inputs may be any that keep to these rules, and one draw needn't show every extreme that they name: `selected`: the 64 indices of a group are distinct and increasing.
All inputs are finite; a program needn't handle non-finite values.
Results may differ from a plain program's by a relative error of at most 0.011.
Values may be sent and summed in bfloat16 or wider, within the bound.
A program may use at most 128 MiB of HBM per device.

v0:
```python
import functools

import jax
import jax.numpy as jnp
import numpy as np
from jax import lax
from jax.experimental import pallas as pl
from jax.experimental.pallas import tpu as pltpu
from jax.sharding import PartitionSpec as P

D = 2048
H = 16
DN = 128
DR = 64
DV = 128
LAT = 512
KEY = LAT + DR
GROUP = 512
SEL = 64
BF = jnp.bfloat16
F32 = jnp.float32
MESH = pl.DeviceIdType.MESH
EXP_SCALE = float((DN + DR) ** (-0.5) * np.log2(np.e))
COPIES = 96
STAGES = (((0, 0), (0, 1)), ((-1, 0), (1, 1)), ((-1, 1), (1, 0)), ((2, 0), (2, 1)))


def nt(a, b):
    return lax.dot_general(a, b, (((1,), (1,)), ((), ())), preferred_element_type=F32)


def kernel(
    q_ref, fresh_ref, cache_ref, sel_ref, pos_ref, gain_ref, kv_ref, ow_ref, freq_ref,
    att_out, bl_out,
    kbuf, qmsg, qrecv, selmsg, selrecv, kk, kvv, wbuf, qa, qr, qpl, m_s, l_s, acc, hall, omsg, att,
    ssem, rsem, lsem,
):
    g = lax.axis_index("group")
    p = lax.axis_index("prompt")
    x, c = lax.div(g, 2), lax.rem(g, 2)
    z, y = lax.div(p, 4), lax.rem(p, 4)
    other = 1 - c
    used = [0]

    def remote(src, dst, to):
        n = used[0]
        used[0] += 1
        return pltpu.make_async_remote_copy(
            src_ref=src,
            dst_ref=dst,
            send_sem=ssem.at[n],
            recv_sem=rsem.at[n],
            device_id=to,
            device_id_type=MESH,
        )

    def in_group(d):
        return {"group": lax.rem(g + d, 8)}

    def chip(dx):
        return lax.rem(x + dx + 4, 4)

    def peer(dx):
        return {"group": chip(dx) * 2 + c}

    sibling = {"group": x * 2 + other}

    def along_z(d):
        return {"prompt": lax.rem(z + d, 8) * 4 + y}

    def along_y(d):
        return {"prompt": z * 4 + lax.rem(y + d, 4)}

    barrier = pltpu.get_barrier_semaphore()
    everyone = [in_group(d) for d in range(1, 8)]
    everyone += [along_z(d) for d in range(1, 8)] + [along_y(d) for d in range(1, 4)]
    for to in everyone:
        pl.semaphore_signal(barrier, inc=1, device_id=to, device_id_type=MESH)

    part = kv_ref[:, pl.ds(pl.multiple_of(g * 512, 512), 512)]
    kk[z, y] = jnp.concatenate([part[:, :128], part[:, 256:384]], axis=1)
    kvv[z, y] = jnp.concatenate([part[:, 128:256], part[:, 384:]], axis=1)
    wbuf[z, y] = ow_ref[:, pl.ds(pl.multiple_of(g * 256, 256), 256)]

    sel_row = sel_ref[...].astype(F32)
    eye = lax.broadcasted_iota(jnp.int32, (SEL, 128), 0) == lax.broadcasted_iota(
        jnp.int32, (SEL, 128), 1
    )
    selmsg[...] = sel_row
    sel_col = jnp.sum(jnp.where(eye, sel_row, 0.0), -1, keepdims=True)
    place = sel_col + (pos_ref[0, g] * GROUP).astype(F32)
    angles = place * freq_ref[...]
    cosine = jnp.cos(angles)
    lane = lax.broadcasted_iota(jnp.int32, (SEL, 128), 1)
    first = lax.rem(lane, 64) < 32
    low = lane < 64
    sine = jnp.sin(angles)
    sine = jnp.where(first, -sine, sine)

    def rotate(v):
        partner = jnp.where(first, pltpu.roll(v, 96, 1), pltpu.roll(v, 32, 1))
        return v * cosine + partner * sine

    for j in range(8):
        t0 = q_ref[:, j * 384 : j * 384 + 128]
        t1 = q_ref[:, j * 384 + 128 : j * 384 + 256].astype(F32)
        t2 = q_ref[:, j * 384 + 256 : j * 384 + 384].astype(F32)
        qmsg[j, :, :128] = t0
        second = jnp.where(low, pltpu.roll(t1, 64, 1), pltpu.roll(t2, 64, 1))
        qmsg[j, :, 128:256] = second.astype(BF)
        qmsg[j, :, 256:] = rotate(jnp.where(low, t1, t2)).astype(BF)

    pl.semaphore_wait(barrier, len(everyone))

    def gather_z(buf):
        return [remote(buf.at[z, y], buf.at[z, y], along_z(d)) for d in range(1, 8)]

    def gather_y(buf):
        return [remote(buf.at[:, y], buf.at[:, y], along_y(d)) for d in range(1, 4)]

    def start(copies):
        for copy in copies:
            copy.start()

    def received(copies):
        for copy in copies:
            copy.wait_recv()

    kk_z = gather_z(kk)
    start(kk_z)
    sends = list(kk_z)
    order = (4, 3, 5, 2, 6, 1, 7)
    sel_copies = [remote(selmsg, selrecv.at[g], in_group(d)) for d in order]
    start(sel_copies)
    q_copies = [remote(qmsg.at[lax.rem(g + d, 8)], qrecv.at[g], in_group(d)) for d in order]
    start(q_copies)
    sends += sel_copies + q_copies
    qrecv[g] = qmsg[g]
    selrecv[g] = selmsg[...]

    latent = fresh_ref[:, :LAT].astype(F32)
    factor = lax.rsqrt(jnp.mean(latent * latent, -1, keepdims=True) + 1e-06)
    normed = (latent * factor * gain_ref[...].astype(F32)).astype(BF)
    tail = fresh_ref[:, LAT:].astype(F32)
    turned = rotate(jnp.concatenate([tail, tail], axis=1)).astype(BF)
    columns = lax.broadcasted_iota(jnp.int32, (SEL, GROUP), 1).astype(F32)
    hit = (columns == sel_col).astype(F32)
    taken = jnp.max(hit, 0, keepdims=True) > 0.5
    hit = hit.astype(BF)

    def tn(a, b):
        return lax.dot_general(a, b, (((0,), (0,)), ((), ())), preferred_element_type=F32)

    top = jnp.where(taken, tn(normed, hit), cache_ref[:LAT, :].astype(F32)).astype(BF)
    bottom = jnp.where(taken, tn(turned, hit)[:DR], cache_ref[LAT:, :].astype(F32)).astype(BF)
    for half in range(2):
        cols = slice(half * 256, half * 256 + 256)
        kbuf[0, half, c, :LAT, :] = top[:, cols]
        kbuf[0, half, c, LAT:, :] = bottom[:, cols]

    own = [kbuf.at[0, half, c] for half in range(2)]
    to_sib = [remote(own[i], kbuf.at[0, i, c], sibling) for i in range(2)]
    right = [remote(own[0], kbuf.at[1, 0, c], peer(1)), remote(own[1], kbuf.at[2, 0, c], peer(1))]
    left = [remote(own[1], kbuf.at[1, 1, c], peer(-1)), remote(own[0], kbuf.at[2, 1, c], peer(-1))]
    start([right[0], left[0], to_sib[0], to_sib[1], right[1], left[1]])
    sends += to_sib + right + left
    to_hbm = [
        pltpu.make_async_copy(own[i], bl_out.at[:, pl.ds(i * 256, 256)], lsem.at[i])
        for i in range(2)
    ]
    start(to_hbm)

    kvv_z = gather_z(kvv)
    start(kvv_z)
    w_z = gather_z(wbuf)
    start(w_z)
    sends += kvv_z + w_z

    m_s[...] = jnp.full(m_s.shape, -1e30, F32)
    l_s[...] = jnp.zeros(l_s.shape, F32)
    acc[...] = jnp.zeros(acc.shape, F32)

    received(kk_z)
    kk_y = gather_y(kk)
    start(kk_y)
    sends += kk_y
    received(sel_copies)
    for src in range(8):
        column = jnp.sum(jnp.where(eye, selrecv[src], 0.0), -1, keepdims=True)
        column = column + (pos_ref[0, src] * GROUP).astype(F32)
        qpl[src * SEL : src * SEL + SEL, :] = column
        qpl[512 + src * SEL : 512 + src * SEL + SEL, :] = column
    received(q_copies)
    for src in range(8):
        pair = qrecv[src, :, 256:].astype(F32)
        qr[src * SEL : src * SEL + SEL, :] = pair[:, :DR].astype(BF)
        qr[512 + src * SEL : 512 + src * SEL + SEL, :] = pltpu.roll(pair, 64, 1)[:, :DR].astype(BF)
    received(kk_y)
    for head in range(2):
        lanes = slice(head * 128, head * 128 + 128)
        keys = kk[:, :, :, lanes].reshape(LAT, DN)
        plain = qrecv[:, :, lanes].reshape(512, DN)
        qa[head * 512 : head * 512 + 512, :] = nt(plain, keys).astype(BF)

    def attend(stage, core, head, last):
        rows = pl.ds(head * 512, 512) if isinstance(head, int) else pl.ds(pl.multiple_of(head * 512, 512), 512)
        place = qpl[rows, :]
        number = lax.broadcasted_iota(jnp.int32, (512, 256), 1).astype(F32)
        query, turned = qa[rows, :], qr[rows, :]
        scores = []
        for i, (dx, half) in enumerate(STAGES[stage]):
            base = pos_ref[0, chip(dx) * 2 + core] * GROUP + half * 256
            s = jnp.dot(query, kbuf[stage, i, core, :LAT, :], preferred_element_type=F32)
            s += jnp.dot(turned, kbuf[stage, i, core, LAT:, :], preferred_element_type=F32)
            scores.append(jnp.where(number <= place - base.astype(F32), s, -1e30))
        peak = jnp.maximum(jnp.max(scores[0], -1, keepdims=True), jnp.max(scores[1], -1, keepdims=True))
        old = m_s[rows, :]
        peak = jnp.maximum(old, peak)
        probs = [jnp.exp2((s - peak) * EXP_SCALE) for s in scores]
        decay = jnp.exp2((old - peak) * EXP_SCALE)
        total = l_s[rows, :] * decay + jnp.sum(probs[0] + probs[1], -1, keepdims=True)
        mixed = acc[rows, :] * decay
        for i in range(2):
            mixed += nt(probs[i].astype(BF), kbuf[stage, i, core, :LAT, :])
        if last:
            return (mixed / total).astype(BF)
        m_s[rows, :] = peak
        l_s[rows, :] = total
        acc[rows, :] = mixed

    def both_heads(stage, core):
        def body(head, carry):
            attend(stage, core, head, False)
            return carry

        lax.fori_loop(0, 2, body, 0)

    both_heads(0, c)
    received(to_sib)
    both_heads(0, other)
    received(kvv_z)
    kvv_y = gather_y(kvv)
    start(kvv_y)
    sends += kvv_y

    received([right[0], left[0]])
    relay = [
        remote(kbuf.at[1, 0, c], kbuf.at[3, 0, c], peer(1)),
        remote(kbuf.at[1, 1, c], kbuf.at[3, 1, c], peer(-1)),
    ]
    start(relay)
    sends += relay
    for stage in range(1, 4):
        if stage == 2:
            received([right[1], left[1]])
        if stage == 3:
            received(relay)
        forward = [remote(kbuf.at[stage, i, c], kbuf.at[stage, i, c], sibling) for i in range(2)]
        start(forward)
        sends += forward
        both_heads(stage, c)
        if stage == 1:
            received(w_z)
            w_y = gather_y(wbuf)
            start(w_y)
            sends += w_y
        received(forward)
        if stage < 3:
            both_heads(stage, other)
    received(kvv_y)

    shares = []
    for head in range(2):
        mix = attend(3, other, head, True)
        lanes = pl.ds(head * 128, 128)
        values = kvv[:, :, :, head * 128 : head * 128 + 128].reshape(LAT, DV)
        hall[g, :, lanes] = jnp.dot(mix, values, preferred_element_type=F32).astype(BF)
        mine = hall.at[g, :, lanes]
        share = [remote(mine, mine, to) for to in (peer(2), peer(1), peer(-1), sibling)]
        start(share)
        sends += share
        shares.append(share)
    passed = []
    for head in range(2):
        lanes = pl.ds(head * 128, 128)
        for i, dx in ((1, -1), (2, 1), (0, 2)):
            shares[head][i].wait_recv()
            got = hall.at[chip(dx) * 2 + c, :, lanes]
            passed.append(remote(got, got, sibling))
            passed[-1].start()
    sends += passed
    received([shares[0][3], shares[1][3]])
    received(w_y)
    received(passed)

    total = jnp.dot(hall[0], wbuf[0].reshape(256, 256), preferred_element_type=F32)
    for i in range(1, 8):
        total += jnp.dot(hall[i], wbuf[i].reshape(256, 256), preferred_element_type=F32)
    omsg[...] = total.astype(BF).reshape(8, SEL, 256)
    cols = pl.ds(pl.multiple_of(g * 256, 256), 256)
    back = [remote(omsg.at[lax.rem(g + d, 8)], att.at[:, cols], in_group(d)) for d in order]
    start(back)
    sends += back
    att[:, cols] = omsg[g]
    received(back)
    out = pltpu.make_async_copy(att, att_out, lsem.at[2])
    out.start()
    for copy in sends:
        copy.wait_send()
    for copy in to_hbm:
        copy.wait()
    out.wait()


def shards(queries, fresh, cache, selected, position, gain, kv_up, out_weight):
    freqs = np.float32(10000.0) ** (-(np.arange(128) % 32).astype(np.float32) / np.float32(32))
    row = jnp.pad(selected.reshape(1, SEL), ((0, 0), (0, 128 - SEL)))
    vmem = pl.BlockSpec(memory_space=pltpu.VMEM)
    smem = pl.BlockSpec(memory_space=pltpu.SMEM)
    hbm = pl.BlockSpec(memory_space=pl.ANY)
    attended, blended = pl.pallas_call(
        kernel,
        name="blend_attend",
        out_shape=(
            jax.ShapeDtypeStruct((SEL, D), BF),
            jax.ShapeDtypeStruct((KEY, GROUP), BF),
        ),
        in_specs=[vmem] * 4 + [smem] + [vmem] * 4,
        out_specs=(hbm, hbm),
        scratch_shapes=[
            pltpu.VMEM((4, 2, 2, KEY, 256), BF),
            pltpu.VMEM((8, SEL, 384), BF),
            pltpu.VMEM((8, SEL, 384), BF),
            pltpu.VMEM((1, 128), F32),
            pltpu.VMEM((8, 1, 128), F32),
            pltpu.VMEM((8, 4, 16, 256), BF),
            pltpu.VMEM((8, 4, 16, 256), BF),
            pltpu.VMEM((8, 4, 64, 256), BF),
            pltpu.VMEM((1024, LAT), BF),
            pltpu.VMEM((1024, DR), BF),
            pltpu.VMEM((1024, 1), F32),
            pltpu.VMEM((1024, 1), F32),
            pltpu.VMEM((1024, 1), F32),
            pltpu.VMEM((1024, LAT), F32),
            pltpu.VMEM((8, 512, 256), BF),
            pltpu.VMEM((8, SEL, 256), BF),
            pltpu.VMEM((SEL, D), BF),
            pltpu.SemaphoreType.DMA((COPIES,)),
            pltpu.SemaphoreType.DMA((COPIES,)),
            pltpu.SemaphoreType.DMA((3,)),
        ],
        compiler_params=pltpu.CompilerParams(
            collective_id=0, has_side_effects=True, vmem_limit_bytes=56 << 20
        ),
    )(
        queries.reshape(SEL, H * (DN + DR)),
        fresh.reshape(SEL, KEY),
        jnp.swapaxes(cache.reshape(GROUP, KEY), 0, 1),
        row,
        position,
        gain.reshape(1, LAT),
        kv_up,
        out_weight,
        jnp.asarray(freqs.reshape(1, 128)),
    )
    blended = jnp.swapaxes(blended, 0, 1).reshape(1, 1, GROUP, KEY)
    return attended.reshape(1, 1, SEL, D), blended


def solution(mesh):
    return jax.shard_map(
        shards,
        mesh=mesh,
        in_specs=(
            P("prompt", "group", None, None),
            P("prompt", "group", None, None),
            P("prompt", "group", None, None),
            P("prompt", "group", None),
            P("prompt", None),
            P(),
            P("prompt", None),
            P("prompt", None),
        ),
        out_specs=(P("prompt", "group", None, None), P("prompt", "group", None, None)),
        check_vma=False,
    )
```

profile of v0, /device:TPU:1, one launch (start us, length us, event | category | flops | bytes accessed | tf_op | source)
XLA Modules:
  0.0 70.8 jit_solution(5011225542926370847)
XLA Ops:
  0.6 0.0 copy-start.1
  0.6 0.6 copy-done.1
  1.3 0.0 copy-start
  1.3 0.5 pad.4.sel_ref
  1.8 0.2 copy-done
  2.0 0.6 reshape.29.gain_ref
  2.5 64.7 %blend_attend.1 = (bf16[64,2048]{1,0:T(8,128)(2,1)}, bf16[576,512]{1,0:T(8,128)(2,1)}) custom-call(bf16[64,3072]{1,0:T(8,128)(2,1)} %bitcast.12, bf16[64,576]{1,0:T(8,128)(2,1)} %bitcast.14, bf16[576,512]{1,0:T(8,128)(2,1)} %bitcast.10, s32[1,128]{1,0:T(1,128)} %pad.4.sel_ref, s32[1,8]{1,0:T(1,128)} %pos_ref.1, bf16[1,512]{1,0:T(2,128)(2,1)} %reshape.29.gain_ref, ...), custom_call_target="tpu_custom_call" | custom-call | tf_op jit(solution)/shard_map/blend_attend/pallas_call | solution.py:321
  67.2 1.7 %copy.13 = bf16[1,1,64,2048]{3,2,1,0:T(8,128)(2,1)} copy(bf16[1,1,64,2048]{3,2,1,0:T(8,128)(2,1)} %bitcast.13) | data formatting | bytes 524288
  68.9 1.9 %copy.14 = bf16[1,1,512,576]{2,3,1,0:T(8,128)(2,1)} copy(bf16[1,1,512,576]{2,3,1,0:T(8,128)(2,1)} %bitcast.11) | data formatting | bytes 1179648
Async XLA Ops:
  0.6 0.7 copy-start.1
  1.3 0.7 copy-start
where the time goes:
time: 71 us; the launch traced here: 70.8 us
  Pallas kernels  64.7 us (91%)
  local copies, waits for them, and re-layouts  5.49 us (8%)
    pallas_call x1, Pallas kernels, shards(): pl.pallas_call(kernel, name='blend_attend', out_shape=(jax.ShapeDtypeStru...  64.7 us
    unnamed x6, local copies, waits for them, and re-layouts  4.4 us

commit v1 on v0

--- a/solution.py
+++ b/solution.py
@@ -32,7 +32,7 @@
 def kernel(
     q_ref, fresh_ref, cache_ref, sel_ref, pos_ref, gain_ref, kv_ref, ow_ref, freq_ref,
     att_out, bl_out,
-    kbuf, qmsg, qrecv, selmsg, selrecv, kk, kvv, wbuf, qa, qr, qpl, m_s, l_s, acc, hall, omsg, att,
+    kbuf, qmsg, qrecv, selmsg, selrecv, kk, kvv, wa, wb, qa, qr, qpl, m_s, l_s, acc, hd, hall, ob, land,
     ssem, rsem, lsem,
 ):
     g = lax.axis_index("group")
@@ -80,13 +80,15 @@
     part = kv_ref[:, pl.ds(pl.multiple_of(g * 512, 512), 512)]
     kk[z, y] = jnp.concatenate([part[:, :128], part[:, 256:384]], axis=1)
     kvv[z, y] = jnp.concatenate([part[:, 128:256], part[:, 384:]], axis=1)
-    wbuf[z, y] = ow_ref[:, pl.ds(pl.multiple_of(g * 256, 256), 256)]
+    wa[z, y] = ow_ref[:, pl.ds(pl.multiple_of(c * 1024, 1024), 512)]
+    wb[z, y] = ow_ref[:, pl.ds(pl.multiple_of(c * 1024 + 512, 512), 512)]
 
     sel_row = sel_ref[...].astype(F32)
-    eye = lax.broadcasted_iota(jnp.int32, (SEL, 128), 0) == lax.broadcasted_iota(
-        jnp.int32, (SEL, 128), 1
+    eye = lax.broadcasted_iota(jnp.int32, (SEL, SEL), 0) == lax.broadcasted_iota(
+        jnp.int32, (SEL, SEL), 1
     )
-    selmsg[...] = sel_row
+    selmsg[...] = jnp.zeros(selmsg.shape, F32)
+    selmsg[:, :SEL] = sel_row
     sel_col = jnp.sum(jnp.where(eye, sel_row, 0.0), -1, keepdims=True)
     place = sel_col + (pos_ref[0, g] * GROUP).astype(F32)
     angles = place * freq_ref[...]
@@ -126,21 +128,34 @@
         for copy in copies:
             copy.wait_recv()
 
+    def ring(buf, lead, k):
+        up, down = lax.rem(z - k + 9, 8), lax.rem(z + k - 1, 8)
+        if k < 4:
+            pair = (buf.at[(up, *lead)], buf.at[(down, *lead)])
+        else:
+            n = buf.shape[1 + len(lead)] // 2
+            pair = (buf.at[(up, *lead, pl.ds(0, n))], buf.at[(down, *lead, pl.ds(n, n))])
+        return [remote(pair[0], pair[0], along_z(1)), remote(pair[1], pair[1], along_z(7))]
+
     kk_z = gather_z(kk)
     start(kk_z)
     sends = list(kk_z)
+    wa_y = [remote(wa.at[z, y], wa.at[z, y], along_y(d)) for d in range(1, 4)]
+    b_step = ring(wb, (y,), 1)
     order = (4, 3, 5, 2, 6, 1, 7)
     sel_copies = [remote(selmsg, selrecv.at[g], in_group(d)) for d in order]
     start(sel_copies)
     q_copies = [remote(qmsg.at[lax.rem(g + d, 8)], qrecv.at[g], in_group(d)) for d in order]
     start(q_copies)
-    sends += sel_copies + q_copies
+    kvv_z = gather_z(kvv)
+    start(b_step + wa_y + kvv_z)
+    sends += sel_copies + q_copies + b_step + wa_y + kvv_z
     qrecv[g] = qmsg[g]
     selrecv[g] = selmsg[...]
 
     latent = fresh_ref[:, :LAT].astype(F32)
     factor = lax.rsqrt(jnp.mean(latent * latent, -1, keepdims=True) + 1e-06)
-    normed = (latent * factor * gain_ref[...].astype(F32)).astype(BF)
+    normed = (latent * factor * gain_ref[...].astype(F32).reshape(1, LAT)).astype(BF)
     tail = fresh_ref[:, LAT:].astype(F32)
     turned = rotate(jnp.concatenate([tail, tail], axis=1)).astype(BF)
     columns = lax.broadcasted_iota(jnp.int32, (SEL, GROUP), 1).astype(F32)
@@ -170,12 +185,6 @@
     ]
     start(to_hbm)
 
-    kvv_z = gather_z(kvv)
-    start(kvv_z)
-    w_z = gather_z(wbuf)
-    start(w_z)
-    sends += kvv_z + w_z
-
     m_s[...] = jnp.full(m_s.shape, -1e30, F32)
     l_s[...] = jnp.zeros(l_s.shape, F32)
     acc[...] = jnp.zeros(acc.shape, F32)
@@ -184,29 +193,51 @@
     kk_y = gather_y(kk)
     start(kk_y)
     sends += kk_y
+
+    def pass_on(buf, lead, k, step):
+        received(step)
+        step = ring(buf, lead, k)
+        start(step)
+        sends.extend(step)
+        return step
+
+    b_step = pass_on(wb, (y,), 2, b_step)
+    a_step = pass_on(wa, (), 1, wa_y)
+    received(kvv_z)
+    kvv_y = gather_y(kvv)
+    start(kvv_y)
+    sends += kvv_y
     received(sel_copies)
+
+    def row_of(src, head):
+        at = (src // 2) * 256 + head * 128 + (src % 2) * SEL
+        return slice(at, at + SEL)
+
     for src in range(8):
-        column = jnp.sum(jnp.where(eye, selrecv[src], 0.0), -1, keepdims=True)
+        column = jnp.sum(jnp.where(eye, selrecv[src][:, :SEL], 0.0), -1, keepdims=True)
         column = column + (pos_ref[0, src] * GROUP).astype(F32)
-        qpl[src * SEL : src * SEL + SEL, :] = column
-        qpl[512 + src * SEL : 512 + src * SEL + SEL, :] = column
+        for head in range(2):
+            qpl[row_of(src, head), :] = column
+    b_step = pass_on(wb, (y,), 3, b_step)
     received(q_copies)
     for src in range(8):
         pair = qrecv[src, :, 256:].astype(F32)
-        qr[src * SEL : src * SEL + SEL, :] = pair[:, :DR].astype(BF)
-        qr[512 + src * SEL : 512 + src * SEL + SEL, :] = pltpu.roll(pair, 64, 1)[:, :DR].astype(BF)
+        qr[row_of(src, 0), :] = pair[:, :DR].astype(BF)
+        qr[row_of(src, 1), :] = pltpu.roll(pair, 64, 1)[:, :DR].astype(BF)
     received(kk_y)
     for head in range(2):
         lanes = slice(head * 128, head * 128 + 128)
         keys = kk[:, :, :, lanes].reshape(LAT, DN)
         plain = qrecv[:, :, lanes].reshape(512, DN)
-        qa[head * 512 : head * 512 + 512, :] = nt(plain, keys).astype(BF)
-
-    def attend(stage, core, head, last):
-        rows = pl.ds(head * 512, 512) if isinstance(head, int) else pl.ds(pl.multiple_of(head * 512, 512), 512)
+        qa[:, head] = nt(plain, keys).astype(BF).reshape(4, 128, LAT)
+    b_step = pass_on(wb, (y,), 4, b_step)
+
+    def attend(stage, core, at, count, last):
+        size = count * 256
+        rows = pl.ds(pl.multiple_of(at * 256, 256), size)
         place = qpl[rows, :]
-        number = lax.broadcasted_iota(jnp.int32, (512, 256), 1).astype(F32)
-        query, turned = qa[rows, :], qr[rows, :]
+        number = lax.broadcasted_iota(jnp.int32, (size, 256), 1).astype(F32)
+        query, turned = qa[pl.ds(at, count)].reshape(size, LAT), qr[rows, :]
         scores = []
         for i, (dx, half) in enumerate(STAGES[stage]):
             base = pos_ref[0, chip(dx) * 2 + core] * GROUP + half * 256
@@ -228,20 +259,21 @@
         l_s[rows, :] = total
         acc[rows, :] = mixed
 
-    def both_heads(stage, core):
-        def body(head, carry):
-            attend(stage, core, head, False)
+    def step(stage, core):
+        def body(tile, carry):
+            attend(stage, core, tile * 2, 2, False)
             return carry
 
         lax.fori_loop(0, 2, body, 0)
 
-    both_heads(0, c)
+    step(0, c)
     received(to_sib)
-    both_heads(0, other)
-    received(kvv_z)
-    kvv_y = gather_y(kvv)
-    start(kvv_y)
-    sends += kvv_y
+    received(b_step)
+    wb_y = gather_y(wb)
+    start(wb_y)
+    sends += wb_y
+    a_step = pass_on(wa, (), 2, a_step)
+    step(0, other)
 
     received([right[0], left[0]])
     relay = [
@@ -258,63 +290,67 @@
         forward = [remote(kbuf.at[stage, i, c], kbuf.at[stage, i, c], sibling) for i in range(2)]
         start(forward)
         sends += forward
-        both_heads(stage, c)
-        if stage == 1:
-            received(w_z)
-            w_y = gather_y(wbuf)
-            start(w_y)
-            sends += w_y
+        step(stage, c)
+        if stage < 3:
+            a_step = pass_on(wa, (), stage + 2, a_step)
         received(forward)
         if stage < 3:
-            both_heads(stage, other)
+            step(stage, other)
     received(kvv_y)
 
+    values = [kvv[:, :, :, head * 128 : head * 128 + 128].reshape(LAT, DV) for head in range(2)]
     shares = []
-    for head in range(2):
-        mix = attend(3, other, head, True)
-        lanes = pl.ds(head * 128, 128)
-        values = kvv[:, :, :, head * 128 : head * 128 + 128].reshape(LAT, DV)
-        hall[g, :, lanes] = jnp.dot(mix, values, preferred_element_type=F32).astype(BF)
-        mine = hall.at[g, :, lanes]
-        share = [remote(mine, mine, to) for to in (peer(2), peer(1), peer(-1), sibling)]
-        start(share)
-        sends += share
-        shares.append(share)
+    for i, dx in enumerate((2, 1, -1, 0)):
+        mix = attend(3, other, chip(dx), 1, True)
+        heads = [
+            jnp.dot(mix[head * 128 : head * 128 + 128], values[head], preferred_element_type=F32)
+            for head in range(2)
+        ]
+        heads = jnp.concatenate(heads, axis=1).astype(BF)
+        if dx:
+            hd[i] = heads
+            shares.append(remote(hd.at[i], hall.at[g], peer(dx)))
+        else:
+            hall[g] = heads
+            shares.append(remote(hall.at[g], hall.at[g], sibling))
+        shares[-1].start()
+    sends += shares
     passed = []
-    for head in range(2):
-        lanes = pl.ds(head * 128, 128)
-        for i, dx in ((1, -1), (2, 1), (0, 2)):
-            shares[head][i].wait_recv()
-            got = hall.at[chip(dx) * 2 + c, :, lanes]
-            passed.append(remote(got, got, sibling))
-            passed[-1].start()
+    for i, dx in enumerate((2, 1, -1)):
+        shares[i].wait_recv()
+        got = hall.at[chip(-dx) * 2 + c]
+        passed.append(remote(got, got, sibling))
+        passed[-1].start()
     sends += passed
-    received([shares[0][3], shares[1][3]])
-    received(w_y)
-    received(passed)
-
-    total = jnp.dot(hall[0], wbuf[0].reshape(256, 256), preferred_element_type=F32)
-    for i in range(1, 8):
-        total += jnp.dot(hall[i], wbuf[i].reshape(256, 256), preferred_element_type=F32)
-    omsg[...] = total.astype(BF).reshape(8, SEL, 256)
-    cols = pl.ds(pl.multiple_of(g * 256, 256), 256)
-    back = [remote(omsg.at[lax.rem(g + d, 8)], att.at[:, cols], in_group(d)) for d in order]
-    start(back)
+    received(a_step + wb_y)
+    received(shares[3:] + passed)
+
+    outs = []
+    back = []
+    for n, weight in enumerate((wa, wb)):
+        total = jnp.dot(hall[0], weight[0].reshape(256, 512), preferred_element_type=F32)
+        for i in range(1, 8):
+            total += jnp.dot(hall[i], weight[i].reshape(256, 512), preferred_element_type=F32)
+        ob[n] = total.astype(BF).reshape(2, SEL, 512)
+        back.append(remote(ob.at[n, other], land.at[n], sibling))
+        back[-1].start()
+        cols = pl.ds(pl.multiple_of(c * 1024 + n * 512, 512), 512)
+        outs.append(pltpu.make_async_copy(ob.at[n, c], att_out.at[:, cols], lsem.at[2 + n]))
+        outs[-1].start()
     sends += back
-    att[:, cols] = omsg[g]
-    received(back)
-    out = pltpu.make_async_copy(att, att_out, lsem.at[2])
-    out.start()
+    for n in range(2):
+        back[n].wait_recv()
+        cols = pl.ds(pl.multiple_of(other * 1024 + n * 512, 512), 512)
+        outs.append(pltpu.make_async_copy(land.at[n], att_out.at[:, cols], lsem.at[4 + n]))
+        outs[-1].start()
     for copy in sends:
         copy.wait_send()
-    for copy in to_hbm:
+    for copy in to_hbm + outs:
         copy.wait()
-    out.wait()
 
 
 def shards(queries, fresh, cache, selected, position, gain, kv_up, out_weight):
     freqs = np.float32(10000.0) ** (-(np.arange(128) % 32).astype(np.float32) / np.float32(32))
-    row = jnp.pad(selected.reshape(1, SEL), ((0, 0), (0, 128 - SEL)))
     vmem = pl.BlockSpec(memory_space=pltpu.VMEM)
     smem = pl.BlockSpec(memory_space=pltpu.SMEM)
     hbm = pl.BlockSpec(memory_space=pl.ANY)
@@ -335,19 +371,21 @@
             pltpu.VMEM((8, 1, 128), F32),
             pltpu.VMEM((8, 4, 16, 256), BF),
             pltpu.VMEM((8, 4, 16, 256), BF),
-            pltpu.VMEM((8, 4, 64, 256), BF),
-            pltpu.VMEM((1024, LAT), BF),
+            pltpu.VMEM((8, 4, 64, 512), BF),
+            pltpu.VMEM((8, 4, 64, 512), BF),
+            pltpu.VMEM((4, 2, 128, LAT), BF),
             pltpu.VMEM((1024, DR), BF),
             pltpu.VMEM((1024, 1), F32),
             pltpu.VMEM((1024, 1), F32),
             pltpu.VMEM((1024, 1), F32),
             pltpu.VMEM((1024, LAT), F32),
-            pltpu.VMEM((8, 512, 256), BF),
-            pltpu.VMEM((8, SEL, 256), BF),
-            pltpu.VMEM((SEL, D), BF),
+            pltpu.VMEM((3, 128, 256), BF),
+            pltpu.VMEM((8, 128, 256), BF),
+            pltpu.VMEM((2, 2, SEL, 512), BF),
+            pltpu.VMEM((2, SEL, 512), BF),
             pltpu.SemaphoreType.DMA((COPIES,)),
             pltpu.SemaphoreType.DMA((COPIES,)),
-            pltpu.SemaphoreType.DMA((3,)),
+            pltpu.SemaphoreType.DMA((6,)),
         ],
         compiler_params=pltpu.CompilerParams(
             collective_id=0, has_side_effects=True, vmem_limit_bytes=56 << 20
@@ -356,9 +394,9 @@
         queries.reshape(SEL, H * (DN + DR)),
         fresh.reshape(SEL, KEY),
         jnp.swapaxes(cache.reshape(GROUP, KEY), 0, 1),
-        row,
+        selected.reshape(1, SEL),
         position,
-        gain.reshape(1, LAT),
+        gain,
         kv_up,
         out_weight,
         jnp.asarray(freqs.reshape(1, 128)),

time: 71 us -> 63.7 us (0.90)
  Pallas kernels: 64.7 us -> 59.3 us
  local copies, waits for them, and re-layouts: 5.49 us -> 3.59 us
    pallas_call x1, Pallas kernels: 64.7 us -> 59.3 us  [shards(): pl.pallas_call(kernel, name='blend_attend', out_shape=(jax.ShapeDtypeStru...]
    unnamed x6 -> x2, local copies, waits for them, and re-layouts: 4.4 us -> 3.59 us
where the time goes in v1:
time: 63.7 us; the launch traced here: 63.6 us
  Pallas kernels  59.3 us (93%)
  local copies, waits for them, and re-layouts  3.59 us (6%)
  between operations  0.64 us (1%)
    pallas_call x1, Pallas kernels, shards(): pl.pallas_call(kernel, name='blend_attend', out_shape=(jax.ShapeDtypeStru...  59.3 us
    unnamed x2, local copies, waits for them, and re-layouts  3.59 us

profile of v1, /device:TPU:1, one launch (start us, length us, event | category | flops | bytes accessed | tf_op | source)
XLA Modules:
  0.0 63.6 jit_solution(14468584210014433037)
XLA Ops:
  0.6 59.3 %blend_attend.1 = (bf16[64,2048]{1,0:T(8,128)(2,1)}, bf16[576,512]{1,0:T(8,128)(2,1)}) custom-call(bf16[64,3072]{1,0:T(8,128)(2,1)} %bitcast.12, bf16[64,576]{1,0:T(8,128)(2,1)} %bitcast.14, bf16[576,512]{1,0:T(8,128)(2,1)} %bitcast.11, s32[1,64]{1,0:T(1,128)} %bitcast.15, s32[1,8]{1,0:T(1,128)} %pos_ref.1, bf16[512]{0:T(512)(128)(2,1)} %gain_ref.1, ...), custom_call_target="tpu_custom_call" | custom-call | tf_op jit(solution)/shard_map/blend_attend/pallas_call | solution.py:357
  60.0 1.7 %copy.13 = bf16[1,1,64,2048]{3,2,1,0:T(8,128)(2,1)} copy(bf16[1,1,64,2048]{3,2,1,0:T(8,128)(2,1)} %bitcast.13) | data formatting | bytes 524288
  61.6 1.9 %copy.14 = bf16[1,1,512,576]{2,3,1,0:T(8,128)(2,1)} copy(bf16[1,1,512,576]{2,3,1,0:T(8,128)(2,1)} %bitcast.10) | data formatting | bytes 1179648

commit v2 on v1

--- a/solution.py
+++ b/solution.py
@@ -30,8 +30,9 @@
 
 
 def kernel(
-    q_ref, fresh_ref, cache_ref, sel_ref, pos_ref, gain_ref, kv_ref, ow_ref, freq_ref,
+    q_hbm, fresh_hbm, cache_hbm, sel_hbm, pos_hbm, gain_hbm, kv_hbm, ow_hbm, freq_hbm,
     att_out, bl_out,
+    q_ref, fresh_ref, cache_ref, sel_ref, pos_ref, gain_ref, kv_ref, freq_ref,
     kbuf, qmsg, qrecv, selmsg, selrecv, kk, kvv, wa, wb, qa, qr, qpl, m_s, l_s, acc, hd, hall, ob, land,
     ssem, rsem, lsem,
 ):
@@ -77,11 +78,29 @@
     for to in everyone:
         pl.semaphore_signal(barrier, inc=1, device_id=to, device_id_type=MESH)
 
-    part = kv_ref[:, pl.ds(pl.multiple_of(g * 512, 512), 512)]
+    fetches = []
+
+    def fetch(src, dst):
+        fetches.append(pltpu.make_async_copy(src, dst, lsem.at[8 + len(fetches)]))
+        fetches[-1].start()
+        return fetches[-1]
+
+    first_needed = [
+        fetch(kv_hbm.at[:, pl.ds(pl.multiple_of(g * 512, 512), 512)], kv_ref),
+        fetch(sel_hbm, sel_ref),
+        fetch(pos_hbm, pos_ref),
+        fetch(freq_hbm, freq_ref),
+        fetch(q_hbm, q_ref),
+        fetch(ow_hbm.at[:, pl.ds(pl.multiple_of(c * 1024, 1024), 512)], wa.at[z, y]),
+        fetch(ow_hbm.at[:, pl.ds(pl.multiple_of(c * 1024 + 512, 512), 512)], wb.at[z, y]),
+    ]
+    later = [fetch(fresh_hbm, fresh_ref), fetch(gain_hbm, gain_ref), fetch(cache_hbm, cache_ref)]
+    for copy in first_needed:
+        copy.wait()
+
+    part = kv_ref[...]
     kk[z, y] = jnp.concatenate([part[:, :128], part[:, 256:384]], axis=1)
     kvv[z, y] = jnp.concatenate([part[:, 128:256], part[:, 384:]], axis=1)
-    wa[z, y] = ow_ref[:, pl.ds(pl.multiple_of(c * 1024, 1024), 512)]
-    wb[z, y] = ow_ref[:, pl.ds(pl.multiple_of(c * 1024 + 512, 512), 512)]
 
     sel_row = sel_ref[...].astype(F32)
     eye = lax.broadcasted_iota(jnp.int32, (SEL, SEL), 0) == lax.broadcasted_iota(
@@ -153,6 +172,8 @@
     qrecv[g] = qmsg[g]
     selrecv[g] = selmsg[...]
 
+    for copy in later:
+        copy.wait()
     latent = fresh_ref[:, :LAT].astype(F32)
     factor = lax.rsqrt(jnp.mean(latent * latent, -1, keepdims=True) + 1e-06)
     normed = (latent * factor * gain_ref[...].astype(F32).reshape(1, LAT)).astype(BF)
@@ -269,7 +290,13 @@
     step(0, c)
     received(to_sib)
     received(b_step)
-    wb_y = gather_y(wb)
+    before, after = lax.rem(y + 3, 4), lax.rem(y + 1, 4)
+
+    def half_y(column, half, to):
+        piece = wb.at[pl.ds(half * 4, 4), column]
+        return remote(piece, piece, along_y(to))
+
+    wb_y = [half_y(y, 0, 1), half_y(y, 1, 3), half_y(y, 1, 1), half_y(y, 0, 3)]
     start(wb_y)
     sends += wb_y
     a_step = pass_on(wa, (), 2, a_step)
@@ -293,6 +320,11 @@
         step(stage, c)
         if stage < 3:
             a_step = pass_on(wa, (), stage + 2, a_step)
+        if stage == 2:
+            received(wb_y[:2])
+            on_y = [half_y(before, 0, 1), half_y(after, 1, 3)]
+            start(on_y)
+            sends += on_y
         received(forward)
         if stage < 3:
             step(stage, other)
@@ -322,7 +354,7 @@
         passed.append(remote(got, got, sibling))
         passed[-1].start()
     sends += passed
-    received(a_step + wb_y)
+    received(a_step + wb_y[2:] + on_y)
     received(shares[3:] + passed)
 
     outs = []
@@ -351,9 +383,8 @@
 
 def shards(queries, fresh, cache, selected, position, gain, kv_up, out_weight):
     freqs = np.float32(10000.0) ** (-(np.arange(128) % 32).astype(np.float32) / np.float32(32))
-    vmem = pl.BlockSpec(memory_space=pltpu.VMEM)
-    smem = pl.BlockSpec(memory_space=pltpu.SMEM)
-    hbm = pl.BlockSpec(memory_space=pl.ANY)
+    hbm = pl.BlockSpec(memory_space=pltpu.HBM)
+    anywhere = pl.BlockSpec(memory_space=pl.ANY)
     attended, blended = pl.pallas_call(
         kernel,
         name="blend_attend",
@@ -361,9 +392,17 @@
             jax.ShapeDtypeStruct((SEL, D), BF),
             jax.ShapeDtypeStruct((KEY, GROUP), BF),
         ),
-        in_specs=[vmem] * 4 + [smem] + [vmem] * 4,
-        out_specs=(hbm, hbm),
+        in_specs=[hbm] * 9,
+        out_specs=(anywhere, anywhere),
         scratch_shapes=[
+            pltpu.VMEM((SEL, H * (DN + DR)), BF),
+            pltpu.VMEM((SEL, KEY), BF),
+            pltpu.VMEM((KEY, GROUP), BF),
+            pltpu.VMEM((1, SEL), jnp.int32),
+            pltpu.SMEM((1, 8), jnp.int32),
+            pltpu.VMEM((LAT,), BF),
+            pltpu.VMEM((16, 512), BF),
+            pltpu.VMEM((1, 128), F32),
             pltpu.VMEM((4, 2, 2, KEY, 256), BF),
             pltpu.VMEM((8, SEL, 384), BF),
             pltpu.VMEM((8, SEL, 384), BF),
@@ -385,21 +424,26 @@
             pltpu.VMEM((2, SEL, 512), BF),
             pltpu.SemaphoreType.DMA((COPIES,)),
             pltpu.SemaphoreType.DMA((COPIES,)),
-            pltpu.SemaphoreType.DMA((6,)),
+            pltpu.SemaphoreType.DMA((18,)),
         ],
         compiler_params=pltpu.CompilerParams(
-            collective_id=0, has_side_effects=True, vmem_limit_bytes=56 << 20
+            collective_id=0, has_side_effects=True, vmem_limit_bytes=32 << 20
         ),
     )(
-        queries.reshape(SEL, H * (DN + DR)),
-        fresh.reshape(SEL, KEY),
-        jnp.swapaxes(cache.reshape(GROUP, KEY), 0, 1),
-        selected.reshape(1, SEL),
-        position,
-        gain,
-        kv_up,
-        out_weight,
-        jnp.asarray(freqs.reshape(1, 128)),
+        *[
+            pltpu.with_memory_space_constraint(operand, pltpu.HBM)
+            for operand in (
+                queries.reshape(SEL, H * (DN + DR)),
+                fresh.reshape(SEL, KEY),
+                jnp.swapaxes(cache.reshape(GROUP, KEY), 0, 1),
+                selected.reshape(1, SEL),
+                position,
+                gain,
+                kv_up,
+                out_weight,
+                jnp.asarray(freqs.reshape(1, 128)),
+            )
+        ]
     )
     blended = jnp.swapaxes(blended, 0, 1).reshape(1, 1, GROUP, KEY)
     return attended.reshape(1, 1, SEL, D), blended

time: 63.7 us -> 60.3 us (0.947)
  local copies, waits for them, and re-layouts: 3.59 us -> 1.52 us
  Pallas kernels: 59.3 us -> 58 us
    unnamed x2, local copies, waits for them, and re-layouts: 3.59 us -> 1.52 us
    pallas_call x1, Pallas kernels: 59.3 us -> 58 us  [shards(): pl.pallas_call(kernel, name='blend_attend', out_shape=(jax.ShapeDtypeStru...]
where the time goes in v2:
time: 60.3 us; the launch traced here: 60.2 us
  Pallas kernels  58 us (96%)
  local copies, waits for them, and re-layouts  1.52 us (3%)
  between operations  0.64 us (1%)
    pallas_call x1, Pallas kernels, shards(): pl.pallas_call(kernel, name='blend_attend', out_shape=(jax.ShapeDtypeStru...  58 us
    unnamed x2, local copies, waits for them, and re-layouts  1.52 us

profile of v2, /device:TPU:1, one launch (start us, length us, event | category | flops | bytes accessed | tf_op | source)
XLA Modules:
  0.0 60.2 jit_solution(12034602607612246729)
XLA Ops:
  0.6 58.0 %blend_attend.1 = (bf16[64,2048]{1,0:T(8,128)(2,1)S(1)}, bf16[576,512]{1,0:T(8,128)(2,1)S(1)}) custom-call(bf16[64,3072]{1,0:T(8,128)(2,1)} %bitcast.13, bf16[64,576]{1,0:T(8,128)(2,1)} %bitcast.14, bf16[576,512]{1,0:T(8,128)(2,1)} %bitcast.12, s32[1,64]{1,0:T(1,128)} %bitcast.15, s32[1,8]{1,0:T(1,128)} %pos_hbm.1, bf16[512]{0:T(512)(128)(2,1)} %gain_hbm.1, ...), custom_call_target="tpu_custom_call" | custom-call | tf_op jit(solution)/shard_map/blend_attend/pallas_call | solution.py:388
  58.7 0.7 %copy.13 = bf16[1,1,64,2048]{3,2,1,0:T(8,128)(2,1)} copy(bf16[1,1,64,2048]{3,2,1,0:T(8,128)(2,1)S(1)} %bitcast.11) | data formatting | bytes 524288
  59.4 0.8 %copy.14 = bf16[1,1,512,576]{2,3,1,0:T(8,128)(2,1)} copy(bf16[1,1,512,576]{2,3,1,0:T(8,128)(2,1)S(1)} %bitcast.10) | data formatting | bytes 1179648

commit v3 on v2

--- a/solution.py
+++ b/solution.py
@@ -147,20 +147,28 @@
         for copy in copies:
             copy.wait_recv()
 
-    def ring(buf, lead, k):
+    def ring(view, k, half=None):
         up, down = lax.rem(z - k + 9, 8), lax.rem(z + k - 1, 8)
-        if k < 4:
-            pair = (buf.at[(up, *lead)], buf.at[(down, *lead)])
+        if half is not None:
+            pieces = [(view(up, half), 1), (view(down, half), 7)]
+            pieces = pieces if k < 4 else pieces[half : half + 1]
+        elif k < 4:
+            pieces = [(view(up, None), 1), (view(down, None), 7)]
         else:
-            n = buf.shape[1 + len(lead)] // 2
-            pair = (buf.at[(up, *lead, pl.ds(0, n))], buf.at[(down, *lead, pl.ds(n, n))])
-        return [remote(pair[0], pair[0], along_z(1)), remote(pair[1], pair[1], along_z(7))]
+            pieces = [(view(up, 0), 1), (view(down, 1), 7)]
+        return [remote(piece, piece, along_z(d)) for piece, d in pieces]
+
+    def view_a(i, half):
+        return wa.at[i, pl.ds(half * 2, 2)]
+
+    def view_b(i, half):
+        return wb.at[i, y] if half is None else wb.at[i, y, pl.ds(half * 32, 32)]
 
     kk_z = gather_z(kk)
     start(kk_z)
     sends = list(kk_z)
     wa_y = [remote(wa.at[z, y], wa.at[z, y], along_y(d)) for d in range(1, 4)]
-    b_step = ring(wb, (y,), 1)
+    b_step = ring(view_b, 1)
     order = (4, 3, 5, 2, 6, 1, 7)
     sel_copies = [remote(selmsg, selrecv.at[g], in_group(d)) for d in order]
     start(sel_copies)
@@ -215,15 +223,22 @@
     start(kk_y)
     sends += kk_y
 
-    def pass_on(buf, lead, k, step):
+    def pass_b(k, step):
         received(step)
-        step = ring(buf, lead, k)
+        step = ring(view_b, k)
         start(step)
         sends.extend(step)
         return step
 
-    b_step = pass_on(wb, (y,), 2, b_step)
-    a_step = pass_on(wa, (), 1, wa_y)
+    a_steps = [None, None]
+
+    def pass_a(k, half):
+        received(a_steps[half] or [])
+        a_steps[half] = ring(view_a, k, half)
+        start(a_steps[half])
+        sends.extend(a_steps[half])
+
+    b_step = pass_b(2, b_step)
     received(kvv_z)
     kvv_y = gather_y(kvv)
     start(kvv_y)
@@ -239,7 +254,7 @@
         column = column + (pos_ref[0, src] * GROUP).astype(F32)
         for head in range(2):
             qpl[row_of(src, head), :] = column
-    b_step = pass_on(wb, (y,), 3, b_step)
+    b_step = pass_b(3, b_step)
     received(q_copies)
     for src in range(8):
         pair = qrecv[src, :, 256:].astype(F32)
@@ -251,7 +266,10 @@
         keys = kk[:, :, :, lanes].reshape(LAT, DN)
         plain = qrecv[:, :, lanes].reshape(512, DN)
         qa[:, head] = nt(plain, keys).astype(BF).reshape(4, 128, LAT)
-    b_step = pass_on(wb, (y,), 4, b_step)
+    b_step = pass_b(4, b_step)
+    received(wa_y)
+    pass_a(1, 0)
+    pass_a(1, 1)
 
     def attend(stage, core, at, count, last):
         size = count * 256
@@ -299,8 +317,8 @@
     wb_y = [half_y(y, 0, 1), half_y(y, 1, 3), half_y(y, 1, 1), half_y(y, 0, 3)]
     start(wb_y)
     sends += wb_y
-    a_step = pass_on(wa, (), 2, a_step)
     step(0, other)
+    pass_a(2, 0)
 
     received([right[0], left[0]])
     relay = [
@@ -318,16 +336,16 @@
         start(forward)
         sends += forward
         step(stage, c)
+        pass_a(stage + 1, 1)
+        received(forward)
         if stage < 3:
-            a_step = pass_on(wa, (), stage + 2, a_step)
-        if stage == 2:
+            step(stage, other)
+            pass_a(stage + 2, 0)
+        if stage == 1:
             received(wb_y[:2])
             on_y = [half_y(before, 0, 1), half_y(after, 1, 3)]
             start(on_y)
             sends += on_y
-        received(forward)
-        if stage < 3:
-            step(stage, other)
     received(kvv_y)
 
     values = [kvv[:, :, :, head * 128 : head * 128 + 128].reshape(LAT, DV) for head in range(2)]
@@ -347,22 +365,34 @@
             shares.append(remote(hall.at[g], hall.at[g], sibling))
         shares[-1].start()
     sends += shares
+    received(a_steps[0] + a_steps[1] + wb_y[2:] + on_y)
+
+    def project(total, source):
+        part = [
+            jnp.dot(hall[source], weight[source].reshape(256, 512), preferred_element_type=F32)
+            for weight in (wa, wb)
+        ]
+        return part if total is None else [a + b for a, b in zip(total, part)]
+
+    totals = project(None, g)
     passed = []
-    for i, dx in enumerate((2, 1, -1)):
+    for i, dx in ((3, 0), (1, 1), (2, -1), (0, 2)):
         shares[i].wait_recv()
-        got = hall.at[chip(-dx) * 2 + c]
-        passed.append(remote(got, got, sibling))
-        passed[-1].start()
+        if dx:
+            source = chip(-dx) * 2 + c
+            passed.append(remote(hall.at[source], hall.at[source], sibling))
+            passed[-1].start()
+        else:
+            source = x * 2 + other
+        totals = project(totals, source)
     sends += passed
-    received(a_step + wb_y[2:] + on_y)
-    received(shares[3:] + passed)
+    for i, dx in enumerate((1, -1, 2)):
+        passed[i].wait_recv()
+        totals = project(totals, chip(-dx) * 2 + other)
 
     outs = []
     back = []
-    for n, weight in enumerate((wa, wb)):
-        total = jnp.dot(hall[0], weight[0].reshape(256, 512), preferred_element_type=F32)
-        for i in range(1, 8):
-            total += jnp.dot(hall[i], weight[i].reshape(256, 512), preferred_element_type=F32)
+    for n, total in enumerate(totals):
         ob[n] = total.astype(BF).reshape(2, SEL, 512)
         back.append(remote(ob.at[n, other], land.at[n], sibling))
         back[-1].start()

time: 60.3 us -> 56.3 us (0.934)
  Pallas kernels: 58 us -> 54.1 us
    pallas_call x1, Pallas kernels: 58 us -> 54.1 us  [shards(): pl.pallas_call(kernel, name='blend_attend', out_shape=(jax.ShapeDtypeStru...]
where the time goes in v3:
time: 56.3 us; the launch traced here: 56.2 us
  Pallas kernels  54.1 us (96%)
  local copies, waits for them, and re-layouts  1.52 us (3%)
  between operations  0.64 us (1%)
    pallas_call x1, Pallas kernels, shards(): pl.pallas_call(kernel, name='blend_attend', out_shape=(jax.ShapeDtypeStru...  54.1 us
    unnamed x2, local copies, waits for them, and re-layouts  1.52 us

profile of v3, /device:TPU:1, one launch (start us, length us, event | category | flops | bytes accessed | tf_op | source)
XLA Modules:
  0.0 56.2 jit_solution(4533647532143388693)
XLA Ops:
  0.6 54.1 %blend_attend.1 = (bf16[64,2048]{1,0:T(8,128)(2,1)S(1)}, bf16[576,512]{1,0:T(8,128)(2,1)S(1)}) custom-call(bf16[64,3072]{1,0:T(8,128)(2,1)} %bitcast.13, bf16[64,576]{1,0:T(8,128)(2,1)} %bitcast.14, bf16[576,512]{1,0:T(8,128)(2,1)} %bitcast.12, s32[1,64]{1,0:T(1,128)} %bitcast.15, s32[1,8]{1,0:T(1,128)} %pos_hbm.1, bf16[512]{0:T(512)(128)(2,1)} %gain_hbm.1, ...), custom_call_target="tpu_custom_call" | custom-call | tf_op jit(solution)/shard_map/blend_attend/pallas_call | solution.py:418
  54.7 0.7 %copy.13 = bf16[1,1,64,2048]{3,2,1,0:T(8,128)(2,1)} copy(bf16[1,1,64,2048]{3,2,1,0:T(8,128)(2,1)S(1)} %bitcast.11) | data formatting | bytes 524288
  55.4 0.8 %copy.14 = bf16[1,1,512,576]{2,3,1,0:T(8,128)(2,1)} copy(bf16[1,1,512,576]{2,3,1,0:T(8,128)(2,1)S(1)} %bitcast.10) | data formatting | bytes 1179648

commit v4 on v3

--- a/solution.py
+++ b/solution.py
@@ -21,7 +21,7 @@
 F32 = jnp.float32
 MESH = pl.DeviceIdType.MESH
 EXP_SCALE = float((DN + DR) ** (-0.5) * np.log2(np.e))
-COPIES = 96
+COPIES = 112
 STAGES = (((0, 0), (0, 1)), ((-1, 0), (1, 1)), ((-1, 1), (1, 0)), ((2, 0), (2, 1)))
 
 
@@ -74,7 +74,7 @@
 
     barrier = pltpu.get_barrier_semaphore()
     everyone = [in_group(d) for d in range(1, 8)]
-    everyone += [along_z(d) for d in range(1, 8)] + [along_y(d) for d in range(1, 4)]
+    everyone += [along_z(d) for d in (1, 7, 2, 6)] + [along_y(d) for d in range(1, 4)]
     for to in everyone:
         pl.semaphore_signal(barrier, inc=1, device_id=to, device_id_type=MESH)
 
@@ -133,8 +133,12 @@
 
     pl.semaphore_wait(barrier, len(everyone))
 
-    def gather_z(buf):
-        return [remote(buf.at[z, y], buf.at[z, y], along_z(d)) for d in range(1, 8)]
+    def near_z(buf):
+        return [remote(buf.at[z, y], buf.at[z, y], along_z(d)) for d in (1, 7, 2, 6)]
+
+    def far_z(buf):
+        pieces = [(buf.at[lax.rem(z + d, 8), y], to) for d, to in ((7, 2), (1, 6), (6, 2))]
+        return [remote(piece, piece, along_z(to)) for piece, to in pieces]
 
     def gather_y(buf):
         return [remote(buf.at[:, y], buf.at[:, y], along_y(d)) for d in range(1, 4)]
@@ -164,9 +168,9 @@
     def view_b(i, half):
         return wb.at[i, y] if half is None else wb.at[i, y, pl.ds(half * 32, 32)]
 
-    kk_z = gather_z(kk)
-    start(kk_z)
-    sends = list(kk_z)
+    kk_near = near_z(kk)
+    start(kk_near)
+    sends = list(kk_near)
     wa_y = [remote(wa.at[z, y], wa.at[z, y], along_y(d)) for d in range(1, 4)]
     b_step = ring(view_b, 1)
     order = (4, 3, 5, 2, 6, 1, 7)
@@ -174,9 +178,8 @@
     start(sel_copies)
     q_copies = [remote(qmsg.at[lax.rem(g + d, 8)], qrecv.at[g], in_group(d)) for d in order]
     start(q_copies)
-    kvv_z = gather_z(kvv)
-    start(b_step + wa_y + kvv_z)
-    sends += sel_copies + q_copies + b_step + wa_y + kvv_z
+    start(b_step + wa_y)
+    sends += sel_copies + q_copies + b_step + wa_y
     qrecv[g] = qmsg[g]
     selrecv[g] = selmsg[...]
 
@@ -218,10 +221,10 @@
     l_s[...] = jnp.zeros(l_s.shape, F32)
     acc[...] = jnp.zeros(acc.shape, F32)
 
-    received(kk_z)
-    kk_y = gather_y(kk)
-    start(kk_y)
-    sends += kk_y
+    received(kk_near)
+    kk_far = far_z(kk)
+    start(kk_far)
+    sends += kk_far
 
     def pass_b(k, step):
         received(step)
@@ -239,10 +242,40 @@
         sends.extend(a_steps[half])
 
     b_step = pass_b(2, b_step)
-    received(kvv_z)
-    kvv_y = gather_y(kvv)
-    start(kvv_y)
-    sends += kvv_y
+    received(wa_y)
+    pass_a(1, 0)
+    kvv_near = near_z(kvv)
+    start(kvv_near)
+    sends += kvv_near
+    received(kk_far)
+    kk_y = gather_y(kk)
+    start(kk_y)
+    sends += kk_y
+
+    before, after = lax.rem(y + 3, 4), lax.rem(y + 1, 4)
+    y_right, y_left, on_y = {}, {}, []
+
+    def y_piece(column, offset, to):
+        piece = wb.at[lax.rem(z + offset, 8), column]
+        copy = remote(piece, piece, along_y(to))
+        copy.start()
+        sends.append(copy)
+        return copy
+
+    def send_y(right, left):
+        for a, b in zip(right, left):
+            y_right[a] = y_piece(y, a, 1)
+            y_left[b] = y_piece(y, b, 3)
+
+    def relay_y(right, left):
+        for a in right:
+            y_right.pop(a).wait_recv()
+            on_y.append(y_piece(before, a, 1))
+        for b in left:
+            y_left.pop(b).wait_recv()
+            on_y.append(y_piece(after, b, 3))
+
+    send_y((0, 1, 7), (0, 7, 1))
     received(sel_copies)
 
     def row_of(src, head):
@@ -255,6 +288,8 @@
         for head in range(2):
             qpl[row_of(src, head), :] = column
     b_step = pass_b(3, b_step)
+    send_y((2, 6), (6, 2))
+    pass_a(1, 1)
     received(q_copies)
     for src in range(8):
         pair = qrecv[src, :, 256:].astype(F32)
@@ -267,24 +302,33 @@
         plain = qrecv[:, :, lanes].reshape(512, DN)
         qa[:, head] = nt(plain, keys).astype(BF).reshape(4, 128, LAT)
     b_step = pass_b(4, b_step)
-    received(wa_y)
-    pass_a(1, 0)
-    pass_a(1, 1)
-
-    def attend(stage, core, at, count, last):
-        size = count * 256
-        rows = pl.ds(pl.multiple_of(at * 256, 256), size)
+    send_y((3, 5), (5, 3))
+    received(kvv_near)
+    kvv_far = far_z(kvv)
+    start(kvv_far)
+    sends += kvv_far
+    pass_a(2, 0)
+
+    def tile(at):
+        return pl.ds(at * 256 if isinstance(at, int) else pl.multiple_of(at * 256, 256), 256)
+
+    def score(stage, core, at):
+        rows = tile(at)
         place = qpl[rows, :]
-        number = lax.broadcasted_iota(jnp.int32, (size, 256), 1).astype(F32)
-        query, turned = qa[pl.ds(at, count)].reshape(size, LAT), qr[rows, :]
+        number = lax.broadcasted_iota(jnp.int32, (256, 256), 1).astype(F32)
+        query, turned = qa[at].reshape(256, LAT), qr[rows, :]
         scores = []
         for i, (dx, half) in enumerate(STAGES[stage]):
             base = pos_ref[0, chip(dx) * 2 + core] * GROUP + half * 256
             s = jnp.dot(query, kbuf[stage, i, core, :LAT, :], preferred_element_type=F32)
             s += jnp.dot(turned, kbuf[stage, i, core, LAT:, :], preferred_element_type=F32)
             scores.append(jnp.where(number <= place - base.astype(F32), s, -1e30))
-        peak = jnp.maximum(jnp.max(scores[0], -1, keepdims=True), jnp.max(scores[1], -1, keepdims=True))
+        return scores
+
+    def mix(stage, core, at, scores, last):
+        rows = tile(at)
         old = m_s[rows, :]
+        peak = jnp.max(jnp.maximum(scores[0], scores[1]), -1, keepdims=True)
         peak = jnp.maximum(old, peak)
         probs = [jnp.exp2((s - peak) * EXP_SCALE) for s in scores]
         decay = jnp.exp2((old - peak) * EXP_SCALE)
@@ -299,26 +343,23 @@
         acc[rows, :] = mixed
 
     def step(stage, core):
-        def body(tile, carry):
-            attend(stage, core, tile * 2, 2, False)
-            return carry
-
-        lax.fori_loop(0, 2, body, 0)
+        scores = score(stage, core, 0)
+        for at in range(4):
+            ahead = score(stage, core, at + 1) if at < 3 else None
+            mix(stage, core, at, scores, False)
+            scores = ahead
 
     step(0, c)
     received(to_sib)
+    pass_a(2, 1)
+    received(kvv_far)
+    kvv_y = gather_y(kvv)
+    start(kvv_y)
+    sends += kvv_y
+    relay_y((0, 1), (7,))
+    step(0, other)
     received(b_step)
-    before, after = lax.rem(y + 3, 4), lax.rem(y + 1, 4)
-
-    def half_y(column, half, to):
-        piece = wb.at[pl.ds(half * 4, 4), column]
-        return remote(piece, piece, along_y(to))
-
-    wb_y = [half_y(y, 0, 1), half_y(y, 1, 3), half_y(y, 1, 1), half_y(y, 0, 3)]
-    start(wb_y)
-    sends += wb_y
-    step(0, other)
-    pass_a(2, 0)
+    send_y((4,), (4,))
 
     received([right[0], left[0]])
     relay = [
@@ -336,24 +377,27 @@
         start(forward)
         sends += forward
         step(stage, c)
-        pass_a(stage + 1, 1)
+        if stage < 3:
+            pass_a(stage + 2, 0)
+            relay_y(*((((2,), (6,)), ((), (4,)))[stage - 1]))
         received(forward)
         if stage < 3:
             step(stage, other)
-            pass_a(stage + 2, 0)
+            pass_a(stage + 2, 1)
         if stage == 1:
-            received(wb_y[:2])
-            on_y = [half_y(before, 0, 1), half_y(after, 1, 3)]
-            start(on_y)
-            sends += on_y
+            relay_y((3,), (5,))
     received(kvv_y)
 
     values = [kvv[:, :, :, head * 128 : head * 128 + 128].reshape(LAT, DV) for head in range(2)]
     shares = []
-    for i, dx in enumerate((2, 1, -1, 0)):
-        mix = attend(3, other, chip(dx), 1, True)
+    targets = (2, 1, -1, 0)
+    scores = score(3, other, chip(2))
+    for i, dx in enumerate(targets):
+        ahead = score(3, other, chip(targets[i + 1])) if i < 3 else None
+        mixed = mix(3, other, chip(dx), scores, True)
+        scores = ahead
         heads = [
-            jnp.dot(mix[head * 128 : head * 128 + 128], values[head], preferred_element_type=F32)
+            jnp.dot(mixed[head * 128 : head * 128 + 128], values[head], preferred_element_type=F32)
             for head in range(2)
         ]
         heads = jnp.concatenate(heads, axis=1).astype(BF)
@@ -365,7 +409,7 @@
             shares.append(remote(hall.at[g], hall.at[g], sibling))
         shares[-1].start()
     sends += shares
-    received(a_steps[0] + a_steps[1] + wb_y[2:] + on_y)
+    received(a_steps[0] + a_steps[1] + list(y_right.values()) + list(y_left.values()) + on_y)
 
     def project(total, source):
         part = [

time: 56.3 us -> 56.2 us (level)
  no operation moved by 1% of the time
where the time goes in v4:
time: 56.2 us; the launch traced here: 56.1 us
  Pallas kernels  53.9 us (96%)
  local copies, waits for them, and re-layouts  1.52 us (3%)
  between operations  0.64 us (1%)
    pallas_call x1, Pallas kernels, shards(): pl.pallas_call(kernel, name='blend_attend', out_shape=(jax.ShapeDtypeStru...  53.9 us
    unnamed x2, local copies, waits for them, and re-layouts  1.52 us

profile of v4, /device:TPU:1, one launch (start us, length us, event | category | flops | bytes accessed | tf_op | source)
XLA Modules:
  0.0 56.1 jit_solution(2263561745375208490)
XLA Ops:
  0.6 53.9 %blend_attend.1 = (bf16[64,2048]{1,0:T(8,128)(2,1)S(1)}, bf16[576,512]{1,0:T(8,128)(2,1)S(1)}) custom-call(bf16[64,3072]{1,0:T(8,128)(2,1)} %bitcast.13, bf16[64,576]{1,0:T(8,128)(2,1)} %bitcast.14, bf16[576,512]{1,0:T(8,128)(2,1)} %bitcast.12, s32[1,64]{1,0:T(1,128)} %bitcast.15, s32[1,8]{1,0:T(1,128)} %pos_hbm.1, bf16[512]{0:T(512)(128)(2,1)} %gain_hbm.1, ...), custom_call_target="tpu_custom_call" | custom-call | tf_op jit(solution)/shard_map/blend_attend/pallas_call | solution.py:462
  54.6 0.7 %copy.13 = bf16[1,1,64,2048]{3,2,1,0:T(8,128)(2,1)} copy(bf16[1,1,64,2048]{3,2,1,0:T(8,128)(2,1)S(1)} %bitcast.11) | data formatting | bytes 524288
  55.3 0.8 %copy.14 = bf16[1,1,512,576]{2,3,1,0:T(8,128)(2,1)} copy(bf16[1,1,512,576]{2,3,1,0:T(8,128)(2,1)S(1)} %bitcast.10) | data formatting | bytes 1179648
